TPU v7x, 128 devices: a whole 4x4x4 slice. The times are simulated.
128 devices in a mesh: dp: 8 (over z, core), ctx: 16 (over x, y).
Axes of the slice: x: 4, y: 4, z: 4, core: 2. Of those that a mesh axis runs over, the one named last changes fastest.
Arguments:
- tokens: bfloat16 [32768, 2048], P(('dp', 'ctx')), parts along dimension 0, may hold values from -80 to 80
- qkv_weight: bfloat16 [2048, 3072], P('ctx'), may hold values from -0.125 to 0.125
- out_weight: bfloat16 [1024, 2048], P('ctx'), may hold values from -0.1875 to 0.1875
- prior_state: float32 [64, 128, 128], P('dp'), parts along dimension 0, may hold values from -240 to 240
- expert_ids: int32 [32768, 4], P(('dp', 'ctx')), parts along dimension 0, may hold values from 0 to 15, all different within a row; in each aligned block of 256 rows (0 to 255, 256 to 511, ...) at most 96 rows name the same one
- gate_weights: float32 [32768, 4], P(('dp', 'ctx')), parts along dimension 0, may hold values from 0.1 to 1
- expert_in: bfloat16 [16, 2048, 2048], P('ctx'), may hold values from -0.125 to 0.125
- expert_out: bfloat16 [16, 1024, 2048], P('ctx'), may hold values from -0.1875 to 0.1875
Outputs:
- layer_out: bfloat16 [32768, 2048], P(('dp', 'ctx')), parts along dimension 0
There are 8 independent parts, one for each index of `dp`. A program takes and returns all parts, laid end to end along the dimension named above; an argument that names none is the same for every part. Nothing has to cross between parts.
Inputs may be any that keep to these rules, and one draw needn't show every extreme that they name: `expert_ids`: within the 256 rows of one device no expert is named more than 96 times, and in some device's rows some expert is named exactly 96 times.
All inputs are finite; a program needn't handle non-finite values.
Results may differ from a plain program's by a relative error of at most 0.006.
Values may be sent and summed in bfloat16 or wider, within the bound.
No kernel may reach another device: no remote copies, remote signals or barrier semaphores. Data moves between devices by JAX's collectives and lax.ppermute only.
A program may use at most 128 MiB of HBM per device.

v0:
```python
import jax
import jax.numpy as jnp
from jax import lax
from jax.sharding import PartitionSpec as P

HEADS = 8
HD = 128
FF = 1024
EPSILON = 1e-05


def prefix(x, axis, combine, identity):
    length, index = (lax.axis_size(axis), lax.axis_index(axis))
    everything = lax.all_gather(x.astype(jnp.bfloat16), axis)
    start = jnp.broadcast_to(jnp.asarray(identity, x.dtype), x.shape)

    def step(k, before):
        reached = k < index
        new = combine(before, everything[k].astype(x.dtype))
        return jnp.where(reached, new, before)

    return lax.fori_loop(0, length, step, start)


def rms_rows(matrix):
    return matrix * lax.rsqrt(jnp.mean(matrix * matrix, axis=-1, keepdims=True) + EPSILON)


def combine_add(earlier, later):
    return earlier + later


def shards(
    tokens, qkv_weight, out_weight, prior_state, expert_ids, gate_weights, expert_in, expert_out
):
    tok_rows = tokens.shape[0]
    model_width = tokens.shape[1]
    width_heads = HEADS * HD
    groups = lax.axis_size("ctx")
    local_experts = expert_in.shape[0]
    experts = local_experts * groups
    top_count = expert_ids.shape[1]
    capacity = 3 * tok_rows * top_count // (2 * experts)
    normed = rms_rows(tokens.astype(jnp.float32)).astype(jnp.bfloat16)
    columns = normed
    projected = jnp.dot(
        columns,
        lax.all_gather(qkv_weight, "ctx", axis=0, tiled=True),
        preferred_element_type=jnp.float32,
    )
    queries = (
        jax.nn.silu(projected[:, :width_heads]).astype(jnp.bfloat16).reshape(tok_rows, HEADS, HD)
    )
    key_rows = (
        jax.nn.silu(projected[:, width_heads : 2 * width_heads])
        .astype(jnp.bfloat16)
        .reshape(tok_rows, HEADS, HD)
    )
    value_rows = projected[:, 2 * width_heads :].astype(jnp.bfloat16).reshape(tok_rows, HEADS, HD)
    local_state = jnp.einsum(
        "thd,the->hde", key_rows, value_rows, preferred_element_type=jnp.float32
    )
    earlier_sum = prefix(local_state, "ctx", combine_add, jnp.zeros_like(local_state))
    carried = prior_state + earlier_sum
    scores = jnp.einsum("thd,shd->hts", queries, key_rows, preferred_element_type=jnp.float32)
    causal = (
        jnp.arange(tok_rows, dtype=jnp.int32)[:, None]
        >= jnp.arange(tok_rows, dtype=jnp.int32)[None, :]
    )
    scores = jnp.where(causal[None], scores, jnp.float32(0.0)).astype(jnp.bfloat16)
    inside = jnp.einsum("hts,she->the", scores, value_rows, preferred_element_type=jnp.float32)
    from_state = jnp.einsum(
        "thd,hde->the", queries.astype(jnp.float32), carried, precision=lax.Precision.HIGHEST
    )
    head_normed = rms_rows(from_state + inside).astype(jnp.bfloat16).reshape(tok_rows, width_heads)
    columns = head_normed
    attended = jnp.dot(
        columns,
        lax.all_gather(out_weight, "ctx", axis=0, tiled=True),
        preferred_element_type=jnp.float32,
    )
    hidden = (tokens.astype(jnp.float32) + attended).astype(jnp.bfloat16)
    moe_in = rms_rows(hidden.astype(jnp.float32)).astype(jnp.bfloat16)
    flat_ids = expert_ids.reshape(-1)
    onehot = (flat_ids[:, None] == jnp.arange(experts, dtype=jnp.int32)[None, :]).astype(jnp.int32)
    before = jnp.cumsum(onehot, axis=0) - onehot
    slot_index = jnp.sum(before * onehot, axis=1)
    places = flat_ids * capacity + slot_index
    repeated = jnp.repeat(moe_in, top_count, axis=0)
    outgoing = jnp.zeros((experts * capacity, model_width), jnp.bfloat16).at[places].set(repeated)
    outgoing = outgoing.reshape(experts, capacity, model_width)
    arrived = lax.all_to_all(outgoing, "ctx", split_axis=0, concat_axis=0, tiled=True)
    slot_count = arrived.shape[1]
    grouped = arrived.reshape(groups, local_experts, slot_count, model_width)
    gate_up = jnp.einsum("nxid,xdf->nxif", grouped, expert_in, preferred_element_type=jnp.float32)
    middle = (jax.nn.silu(gate_up[..., :FF]) * gate_up[..., FF:]).astype(jnp.bfloat16)
    result = jnp.einsum(
        "nxif,xfd->nxid", middle, expert_out, preferred_element_type=jnp.float32
    ).astype(jnp.bfloat16)
    finished = result.reshape(groups * local_experts, slot_count, model_width)
    returned = lax.all_to_all(finished, "ctx", split_axis=0, concat_axis=0, tiled=True).reshape(
        experts * capacity, model_width
    )
    picked = returned[places].reshape(tok_rows, top_count, model_width).astype(jnp.float32)
    combined = jnp.sum(gate_weights[:, :, None] * picked, axis=1)
    return (hidden.astype(jnp.float32) + combined).astype(jnp.bfloat16)


def solution(mesh):
    return jax.shard_map(
        shards,
        mesh=mesh,
        in_specs=(
            P(("dp", "ctx"), None),
            P("ctx", None),
            P("ctx", None),
            P("dp", None, None),
            P(("dp", "ctx"), None),
            P(("dp", "ctx"), None),
            P("ctx", None, None),
            P("ctx", None, None),
        ),
        out_specs=P(("dp", "ctx"), None),
        check_vma=False,
    )
```

profile of v0, /device:TPU:28, one launch (start us, length us, event | category | flops | bytes accessed | tf_op | source)
XLA Modules:
  0.0 480.7 jit_solution(9268005951179839358)
XLA Ops:
  7.3 1.5 fusion.12
  8.8 91.1 %all-gather.5.cloned.1.call-done = bf16[2048,3072]{1,0:T(8,128)(2,1)} async-done(((bf16[128,3072]{1,0:T(8,128)(2,1)}), bf16[2048,3072]{1,0:T(8,128)(2,1)}) %all-gather.5.cloned.1.call-update) | async-done | bytes 12582928 | tf_op jit(solution)/shard_map/all_gather | solution.py:48
  99.9 6.8 %fusion.20 = f32[256,3072]{1,0:T(8,128)S(1)} fusion(bf16[2048,3072]{1,0:T(8,128)(2,1)} %all-gather.5.cloned.1.call-done, bf16[256,2048]{1,0:T(8,128)(2,1)} %param.10, f32[256]{0:T(256)S(1)} %add_rsqrt_fusion.2), kind=kOutput, calls=%fused_computation.31 | convolution fusion | flops 3222798336 | bytes 16778240 | tf_op jit(solution)/shard_map/dot_general | solution.py:46
  109.8 4.5 reduce-window.6
  115.1 44.8 %all-gather.9.cloned.1.call-done = bf16[128,128,128]{2,1,0:T(8,128)(2,1)} async-done(((bf16[8,128,128]{2,1,0:T(8,128)(2,1)}), bf16[128,128,128]{2,1,0:T(8,128)(2,1)}) %all-gather.9.cloned.1.call-update) | async-done | bytes 4194320 | tf_op jit(solution)/shard_map/all_gather | solution.py:14
  159.9 20.1 %while.14 = (s32[]{:T(128)}, f32[8,128,128]{2,1,0:T(8,128)S(1)}, s32[]{:T(128)}, bf16[16,8,128,128]{3,2,1,0:T(8,128)(2,1)}, s32[]{:T(128)}, /*index=5*/s32[]{:T(128)}) while((s32[]{:T(128)}, f32[8,128,128]{2,1,0:T(8,128)S(1)}, s32[]{:T(128)}, bf16[16,8,128,128]{3,2,1,0:T(8,128)(2,1)}, s32[]{:T(128)}, /*index=5*/s32[]{:T(128)}) %tuple.44), condition=%wide.region_2.3_spmd.clone, body=%wide.region_1.2_spmd.clone.sunk | while | flops 524292 | bytes 1310813 | solution.py:22
  162.5 1.2 add_select_fusion.2
  163.7 1.2 add_select_fusion.2
  165.0 1.2 add_select_fusion.2
  167.5 1.2 add_select_fusion.2
  168.7 1.2 add_select_fusion.2
  170.0 1.2 add_select_fusion.2
  172.5 1.2 add_select_fusion.2
  173.8 1.3 add_select_fusion.2
  177.6 1.2 add_select_fusion.2
  178.9 1.2 add_select_fusion.2
  180.1 1.6 fusion.27
  181.7 2.0 multiply_reduce_fusion.1
  183.8 29.4 %all-gather.7.cloned.1.call-done = bf16[1024,2048]{1,0:T(8,128)(2,1)} async-done(((bf16[64,2048]{1,0:T(8,128)(2,1)}), bf16[1024,2048]{1,0:T(8,128)(2,1)}) %all-gather.7.cloned.1.call-update) | async-done | bytes 4194320 | tf_op jit(solution)/shard_map/all_gather | solution.py:79
  213.2 3.9 fusion.14
  217.4 4.1 broadcast_in_dim.35
  221.5 6.9 %reshape.150 = bf16[1024,2048]{1,0:T(8,128)(2,1)} reshape(bf16[256,4,2048]{2,1,0:T(4,128)(2,1)} %broadcast_in_dim.35) | data formatting | bytes 8388608 | tf_op jit(solution)/shard_map/reshape | solution.py:89
  228.4 11.2 %scatter_custom_fusion = bf16[1536,2048]{1,0:T(8,128)(2,1)} fusion(s32[1024]{0:T(1024)S(1)} %bitcast.85, bf16[1024,2048]{1,0:T(8,128)(2,1)} %reshape.150, bf16[]{:T(256)} %constant.55.clone.1), kind=kCustom, calls=%fused_computation.12 | custom fusion | bytes 6291968 | tf_op jit(solution)/shard_map/scatter | solution.py:90
  239.6 77.4 %all_to_all.10 = bf16[16,96,2048]{2,1,0:T(8,128)(2,1)S(1)} all-to-all(bf16[16,96,2048]{2,1,0:T(8,128)(2,1)} %bitcast.77), channel_id=1, replica_groups=mesh['dp'=8,'ctx'=16] {'ctx'}, dimensions={0} | all-to-all | bytes 12582912 | tf_op jit(solution)/shard_map/all_to_all | solution.py:92
  317.1 16.2 %fusion.3 = f32[16,1,96,2048]{3,2,0,1:T(8,128)S(1)} fusion(bf16[16,96,2048]{2,1,0:T(8,128)(2,1)S(1)} %all_to_all.10, bf16[1,2048,2048]{2,1,0:T(8,128)(2,1)} %param.16), kind=kOutput, calls=%fused_computation.8 | convolution fusion | flops 12884901888 | bytes 27262976 | tf_op jit(solution)/shard_map/nxid,xdf->nxif/dot_general | solution.py:95
  333.3 8.6 %convolution_convert_fusion = bf16[16,96,2048]{2,1,0:T(8,128)(2,1)} fusion(bf16[1,1024,2048]{2,1,0:T(8,128)(2,1)S(1)} %copy-done.3, f32[16,1,96,2048]{3,2,0,1:T(8,128)S(1)} %fusion.3), kind=kOutput, calls=%fused_computation.9 | convolution fusion | flops 6455033856 | bytes 23068672 | tf_op jit(solution)/shard_map/nxif,xfd->nxid/dot_general | solution.py:97
  341.9 8.0 %all-to-all-start.1 = ((bf16[16,96,2048]{2,1,0:T(8,128)(2,1)}), bf16[16,96,2048]{2,1,0:T(8,128)(2,1)}, u32[]{:S(2)}, u32[]{:S(2)}) async-start(bf16[16,96,2048]{2,1,0:T(8,128)(2,1)} %convolution_convert_fusion), calls=%async_computation.1 | async-start | bytes 12582912 | tf_op jit(solution)/shard_map/all_to_all | solution.py:101
  350.1 92.1 %all-to-all-done.1 = bf16[16,96,2048]{2,1,0:T(8,128)(2,1)} async-done(((bf16[16,96,2048]{2,1,0:T(8,128)(2,1)}), bf16[16,96,2048]{2,1,0:T(8,128)(2,1)}, u32[]{:S(2)}, u32[]{:S(2)}) %all-to-all-start.1) | async-done | bytes 6291488 | tf_op jit(solution)/shard_map/all_to_all | solution.py:101
  442.2 12.4 %gather_fusion = bf16[1024,2048]{1,0:T(8,128)(2,1)} fusion(bf16[1536,2048]{1,0:T(8,128)(2,1)} %bitcast.18, s32[1024]{0:T(1024)S(1)} %broadcast_clamp_fusion), kind=kCustom, calls=%fused_computation | custom fusion | bytes 8392704 | tf_op jit(solution)/shard_map/gather | solution.py:104
  454.6 8.3 %reshape.137 = f32[256,4,2048]{2,1,0:T(4,128)} reshape(bf16[1024,2048]{1,0:T(8,128)(2,1)} %gather_fusion) | data formatting | bytes 12582912 | tf_op jit(solution)/shard_map/convert_element_type | solution.py:104
  462.9 10.0 %multiply_reduce_fusion = f32[256,2048]{1,0:T(8,128)S(1)} fusion(f32[256,4,2048]{2,1,0:T(4,128)} %reshape.137, f32[256,4]{1,0:T(8,128)S(1)} %copy.35), kind=kLoop, calls=%fused_computation.5 | loop fusion | flops 3670016 | bytes 10489856 | tf_op jit(solution)/shard_map/reduce_sum | solution.py:105
  472.9 1.3 fusion.16
  (48 shorter events, 12.4 us)
Async XLA Ops:
  6.5 93.4 %all-gather.5.cloned.1.call-start = ((), (), s32[]{:S(2)}) async-start(), calls=%async_computation.2 | async-start | bytes 13369344 | tf_op jit(solution)/shard_map/all_gather | solution.py:48
  7.3 152.7 %all-gather.9.cloned.1.call-start = ((), (), s32[]{:S(2)}) async-start(), calls=%async_computation.4 | async-start | bytes 4456448 | tf_op jit(solution)/shard_map/all_gather | solution.py:14
  106.7 2.7 copy-start.1
  108.7 71.4 %copy-start = (f32[8,128,128]{2,1,0:T(8,128)S(1)}, f32[8,128,128]{2,1,0:T(8,128)}, u32[]{:S(2)}) copy-start(f32[8,128,128]{2,1,0:T(8,128)} %param.13) | copy-start | bytes 1572868
  108.7 104.5 %all-gather.7.cloned.1.call-start = ((), (), s32[]{:S(2)}) async-start(), calls=%async_computation.3 | async-start | bytes 4456448 | tf_op jit(solution)/shard_map/all_gather | solution.py:79
  317.1 16.2 %copy-start.3 = (bf16[1,1024,2048]{2,1,0:T(8,128)(2,1)S(1)}, bf16[1,1024,2048]{2,1,0:T(8,128)(2,1)}, u32[]{:S(2)}) copy-start(bf16[1,1024,2048]{2,1,0:T(8,128)(2,1)} %param.17) | copy-start | bytes 12582916
  341.9 8.0 %copy-start.2 = (f32[256,4]{0,1:T(4,128)S(1)}, f32[256,4]{0,1:T(4,128)}, u32[]{:S(2)}) copy-start(f32[256,4]{0,1:T(4,128)} %param.15) | copy-start | bytes 12292
  341.9 100.3 %all-to-all-start.1 = ((bf16[16,96,2048]{2,1,0:T(8,128)(2,1)}), bf16[16,96,2048]{2,1,0:T(8,128)(2,1)}, u32[]{:S(2)}, u32[]{:S(2)}) async-start(bf16[16,96,2048]{2,1,0:T(8,128)(2,1)} %convolution_convert_fusion), calls=%async_computation.1 | async-start | bytes 12582912 | tf_op jit(solution)/shard_map/all_to_all | solution.py:101
Sparse Core Ops, SparseCore 0:
  9.5 90.3 all-gather.4
  108.8 51.0 all-gather.8
  162.1 51.0 all-gather.6
where the time goes:
time: 482 us; the launch traced here: 481 us
  waiting for transfers between devices  259 us (54%)
  blocking collectives  77.4 us (16%)
  local copies, waits for them, and re-layouts  44.3 us (9%)
  matrix products  40.1 us (8%)
  other arithmetic  38.2 us (8%)
  between operations  13.3 us (3%)
  starting transfers between devices  8.26 us (2%)
    all_to_all x1, waiting for transfers between devices, shards(): lax.all_to_all(finished, 'ctx', split_axis=0, concat_axis=0, tiled=True)  92.1 us
    all_gather x1, waiting for transfers between devices, shards(): lax.all_gather(qkv_weight, 'ctx', axis=0, tiled=True)  91.1 us
    all_to_all x1, blocking collectives, shards(): lax.all_to_all(outgoing, 'ctx', split_axis=0, concat_axis=0, tiled=True)  77.4 us
    all_gather x1, waiting for transfers between devices, prefix(): everything = lax.all_gather(x.astype(jnp.bfloat16), axis)  44.8 us
    all_gather x1, waiting for transfers between devices, shards(): lax.all_gather(out_weight, 'ctx', axis=0, tiled=True)  29.4 us
    select_n x16, other arithmetic, step(): return jnp.where(reached, new, before)  19.8 us
    dot_general x1, matrix products, shards(): jnp.einsum('nxid,xdf->nxif', grouped, expert_in, preferred_element_type=j...  16.2 us
    gather x1, local copies, waits for them, and re-layouts, shards(): returned[places].reshape(tok_rows, top_count, model_width)  12.4 us
  transfers between devices with their start and end apart: 4, of which 4 were waited for; matrix products, arithmetic and copies ran while one was open for 6% of the time, Pallas kernels for 0%

commit v1 on v0

--- a/solution.py
+++ b/solution.py
@@ -7,6 +7,18 @@
 HD = 128
 FF = 1024
 EPSILON = 1e-05
+
+
+def compute_the_frame(vector, device_axis):
+    return jnp.concatenate(
+        jax.lax.all_to_all(
+            jnp.stack([vector for _ in range(jax.lax.psum(1, device_axis))]),
+            device_axis,
+            split_axis=0,
+            concat_axis=0,
+        ),
+        axis=0,
+    )
 
 
 def prefix(x, axis, combine, identity):
@@ -75,9 +87,7 @@
     head_normed = rms_rows(from_state + inside).astype(jnp.bfloat16).reshape(tok_rows, width_heads)
     columns = head_normed
     attended = jnp.dot(
-        columns,
-        lax.all_gather(out_weight, "ctx", axis=0, tiled=True),
-        preferred_element_type=jnp.float32,
+        columns, compute_the_frame(out_weight, "ctx"), preferred_element_type=jnp.float32
     )
     hidden = (tokens.astype(jnp.float32) + attended).astype(jnp.bfloat16)
     moe_in = rms_rows(hidden.astype(jnp.float32)).astype(jnp.bfloat16)

time: 482 us -> 498 us (1.033)
  starting transfers between devices: 8.26 us -> 15.4 us
  waiting for transfers between devices: 259 us -> 265 us
    all_gather x1, waiting for transfers between devices: 44.8 us -> 80.9 us  [prefix(): everything = lax.all_gather(x.astype(jnp.bfloat16), axis)]
    all_gather x1 -> x0, waiting for transfers between devices: 29.4 us -> none  [shards(): lax.all_gather(out_weight, 'ctx', axis=0, tiled=True)]
    all_to_all x0 -> x1, starting transfers between devices: none -> 7.36 us  [compute_the_frame(): jax.lax.all_to_all(jnp.stack([vector for _ in range(jax.lax.psum(1, devic...]
  transfers between devices with their start and end apart: 4 -> 4, of which waited for: 4 -> 3; matrix products, arithmetic and copies ran while one was open for 6% -> 7% of each run, Pallas kernels for 0% -> 0%
where the time goes in v1:
time: 498 us; the launch traced here: 497 us
  waiting for transfers between devices  265 us (53%)
  blocking collectives  77.4 us (16%)
  local copies, waits for them, and re-layouts  46.8 us (9%)
  matrix products  40.1 us (8%)
  other arithmetic  38.2 us (8%)
  starting transfers between devices  15.4 us (3%)
  between operations  13.6 us (3%)
    all_to_all x1, waiting for transfers between devices, shards(): lax.all_to_all(finished, 'ctx', split_axis=0, concat_axis=0, tiled=True)  92.2 us
    all_gather x1, waiting for transfers between devices, shards(): lax.all_gather(qkv_weight, 'ctx', axis=0, tiled=True)  91.1 us
    all_gather x1, waiting for transfers between devices, prefix(): everything = lax.all_gather(x.astype(jnp.bfloat16), axis)  80.9 us
    all_to_all x1, blocking collectives, shards(): lax.all_to_all(outgoing, 'ctx', split_axis=0, concat_axis=0, tiled=True)  77.4 us
    select_n x16, other arithmetic, step(): return jnp.where(reached, new, before)  19.8 us
    dot_general x1, matrix products, shards(): jnp.einsum('nxid,xdf->nxif', grouped, expert_in, preferred_element_type=j...  16.2 us
    gather x1, local copies, waits for them, and re-layouts, shards(): returned[places].reshape(tok_rows, top_count, model_width)  12.4 us
    scatter x1, local copies, waits for them, and re-layouts, shards(): jnp.zeros((experts * capacity, model_width), jnp.bfloat16).at[places]  11.2 us
  transfers between devices with their start and end apart: 4, of which 3 were waited for; matrix products, arithmetic and copies ran while one was open for 7% of the time, Pallas kernels for 0%

profile of v1, /device:TPU:28, one launch (start us, length us, event | category | flops | bytes accessed | tf_op | source)
XLA Modules:
  0.0 496.8 jit_solution(14243297754956165089)
XLA Ops:
  7.3 1.5 fusion.12
  8.8 91.1 %all-gather.4.cloned.1.call-done = bf16[2048,3072]{1,0:T(8,128)(2,1)} async-done(((bf16[128,3072]{1,0:T(8,128)(2,1)}), bf16[2048,3072]{1,0:T(8,128)(2,1)}) %all-gather.4.cloned.1.call-update) | async-done | bytes 12582928 | tf_op jit(solution)/shard_map/all_gather | solution.py:60
  99.9 6.8 %fusion.20 = f32[256,3072]{1,0:T(8,128)S(1)} fusion(bf16[2048,3072]{1,0:T(8,128)(2,1)} %all-gather.4.cloned.1.call-done, bf16[256,2048]{1,0:T(8,128)(2,1)} %param.10, f32[256]{0:T(256)S(1)} %add_rsqrt_fusion.2), kind=kOutput, calls=%fused_computation.31 | convolution fusion | flops 3222798336 | bytes 16778240 | tf_op jit(solution)/shard_map/dot_general | solution.py:58
  108.7 2.5 stack.2
  111.2 7.4 %all-to-all-start = ((bf16[16,64,2048]{2,1,0:T(8,128)(2,1)}), bf16[16,64,2048]{2,1,0:T(8,128)(2,1)}, u32[]{:S(2)}, u32[]{:S(2)}) async-start(bf16[16,64,2048]{2,1,0:T(8,128)(2,1)} %stack.2), calls=%async_computation | async-start | bytes 8388608 | tf_op jit(solution)/shard_map/all_to_all | solution.py:14
  119.0 4.5 reduce-window.6
  124.3 80.9 %all-gather.6.cloned.1.call-done = bf16[128,128,128]{2,1,0:T(8,128)(2,1)} async-done(((bf16[8,128,128]{2,1,0:T(8,128)(2,1)}), bf16[128,128,128]{2,1,0:T(8,128)(2,1)}) %all-gather.6.cloned.1.call-update) | async-done | bytes 4194320 | tf_op jit(solution)/shard_map/all_gather | solution.py:26
  205.1 20.1 %while.14 = (s32[]{:T(128)}, f32[8,128,128]{2,1,0:T(8,128)S(1)}, s32[]{:T(128)}, bf16[16,8,128,128]{3,2,1,0:T(8,128)(2,1)}, s32[]{:T(128)}, /*index=5*/s32[]{:T(128)}) while((s32[]{:T(128)}, f32[8,128,128]{2,1,0:T(8,128)S(1)}, s32[]{:T(128)}, bf16[16,8,128,128]{3,2,1,0:T(8,128)(2,1)}, s32[]{:T(128)}, /*index=5*/s32[]{:T(128)}) %tuple.42), condition=%wide.region_2.3_spmd.clone, body=%wide.region_1.2_spmd.clone.sunk | while | flops 524292 | bytes 1310813 | solution.py:34
  206.4 1.2 add_select_fusion.2
  207.7 1.2 add_select_fusion.2
  208.9 1.2 add_select_fusion.2
  210.2 1.2 add_select_fusion.2
  211.4 1.2 add_select_fusion.2
  212.7 1.2 add_select_fusion.2
  214.0 1.2 add_select_fusion.2
  215.2 1.2 add_select_fusion.2
  217.7 1.2 add_select_fusion.2
  225.3 1.6 fusion.27
  226.9 2.0 multiply_reduce_fusion.1
  229.0 3.9 fusion.14
  233.1 4.1 broadcast_in_dim.35
  237.2 6.9 %reshape.156 = bf16[1024,2048]{1,0:T(8,128)(2,1)} reshape(bf16[256,4,2048]{2,1,0:T(4,128)(2,1)} %broadcast_in_dim.35) | data formatting | bytes 8388608 | tf_op jit(solution)/shard_map/reshape | solution.py:99
  244.1 11.2 %scatter_custom_fusion = bf16[1536,2048]{1,0:T(8,128)(2,1)} fusion(s32[1024]{0:T(1024)S(1)} %bitcast.86, bf16[1024,2048]{1,0:T(8,128)(2,1)} %reshape.156, bf16[]{:T(256)} %constant.55.clone.1), kind=kCustom, calls=%fused_computation.12 | custom fusion | bytes 6291968 | tf_op jit(solution)/shard_map/scatter | solution.py:100
  255.4 77.4 %all_to_all.15 = bf16[16,96,2048]{2,1,0:T(8,128)(2,1)S(1)} all-to-all(bf16[16,96,2048]{2,1,0:T(8,128)(2,1)} %bitcast.78), channel_id=1, replica_groups=mesh['dp'=8,'ctx'=16] {'ctx'}, dimensions={0} | all-to-all | bytes 12582912 | tf_op jit(solution)/shard_map/all_to_all | solution.py:102
  332.8 16.2 %fusion.3 = f32[16,1,96,2048]{3,2,0,1:T(8,128)S(1)} fusion(bf16[16,96,2048]{2,1,0:T(8,128)(2,1)S(1)} %all_to_all.15, bf16[1,2048,2048]{2,1,0:T(8,128)(2,1)} %param.16), kind=kOutput, calls=%fused_computation.8 | convolution fusion | flops 12884901888 | bytes 27262976 | tf_op jit(solution)/shard_map/nxid,xdf->nxif/dot_general | solution.py:105
  349.0 8.6 %convolution_convert_fusion = bf16[16,96,2048]{2,1,0:T(8,128)(2,1)} fusion(bf16[1,1024,2048]{2,1,0:T(8,128)(2,1)S(1)} %copy-done.4, f32[16,1,96,2048]{3,2,0,1:T(8,128)S(1)} %fusion.3), kind=kOutput, calls=%fused_computation.9 | convolution fusion | flops 6455033856 | bytes 23068672 | tf_op jit(solution)/shard_map/nxif,xfd->nxid/dot_general | solution.py:107
  357.6 8.0 %all-to-all-start.2 = ((bf16[16,96,2048]{2,1,0:T(8,128)(2,1)}), bf16[16,96,2048]{2,1,0:T(8,128)(2,1)}, u32[]{:S(2)}, u32[]{:S(2)}) async-start(bf16[16,96,2048]{2,1,0:T(8,128)(2,1)} %convolution_convert_fusion), calls=%async_computation.2 | async-start | bytes 12582912 | tf_op jit(solution)/shard_map/all_to_all | solution.py:111
  365.8 92.2 %all-to-all-done.2 = bf16[16,96,2048]{2,1,0:T(8,128)(2,1)} async-done(((bf16[16,96,2048]{2,1,0:T(8,128)(2,1)}), bf16[16,96,2048]{2,1,0:T(8,128)(2,1)}, u32[]{:S(2)}, u32[]{:S(2)}) %all-to-all-start.2) | async-done | bytes 6291488 | tf_op jit(solution)/shard_map/all_to_all | solution.py:111
  458.0 12.4 %gather_fusion = bf16[1024,2048]{1,0:T(8,128)(2,1)} fusion(bf16[1536,2048]{1,0:T(8,128)(2,1)} %bitcast.19, s32[1024]{0:T(1024)S(1)} %broadcast_clamp_fusion), kind=kCustom, calls=%fused_computation | custom fusion | bytes 8392704 | tf_op jit(solution)/shard_map/gather | solution.py:114
  470.4 8.3 %reshape.143 = f32[256,4,2048]{2,1,0:T(4,128)} reshape(bf16[1024,2048]{1,0:T(8,128)(2,1)} %gather_fusion) | data formatting | bytes 12582912 | tf_op jit(solution)/shard_map/convert_element_type | solution.py:114
  478.7 10.0 %multiply_reduce_fusion = f32[256,2048]{1,0:T(8,128)S(1)} fusion(f32[256,4,2048]{2,1,0:T(4,128)} %reshape.143, f32[256,4]{1,0:T(8,128)S(1)} %copy.35), kind=kLoop, calls=%fused_computation.5 | loop fusion | flops 3670016 | bytes 10489856 | tf_op jit(solution)/shard_map/reduce_sum | solution.py:115
  488.7 1.3 fusion.16
  (50 shorter events, 12.9 us)
Async XLA Ops:
  6.5 93.4 %all-gather.4.cloned.1.call-start = ((), (), s32[]{:S(2)}) async-start(), calls=%async_computation.3 | async-start | bytes 13369344 | tf_op jit(solution)/shard_map/all_gather | solution.py:60
  7.3 197.9 %all-gather.6.cloned.1.call-start = ((), (), s32[]{:S(2)}) async-start(), calls=%async_computation.4 | async-start | bytes 4456448 | tf_op jit(solution)/shard_map/all_gather | solution.py:26
  106.7 1.9 copy-start.1
  111.2 7.4 %copy-start.2 = (s32[256,4]{0,1:T(4,128)S(1)}, s32[256,4]{0,1:T(4,128)}, u32[]{:S(2)}) copy-start(s32[256,4]{0,1:T(4,128)} %param.14) | copy-start | bytes 12292
  111.2 117.8 %all-to-all-start = ((bf16[16,64,2048]{2,1,0:T(8,128)(2,1)}), bf16[16,64,2048]{2,1,0:T(8,128)(2,1)}, u32[]{:S(2)}, u32[]{:S(2)}) async-start(bf16[16,64,2048]{2,1,0:T(8,128)(2,1)} %stack.2), calls=%async_computation | async-start | bytes 8388608 | tf_op jit(solution)/shard_map/all_to_all | solution.py:14
  118.5 106.7 %copy-start = (f32[8,128,128]{2,1,0:T(8,128)S(1)}, f32[8,128,128]{2,1,0:T(8,128)}, u32[]{:S(2)}) copy-start(f32[8,128,128]{2,1,0:T(8,128)} %param.13) | copy-start | bytes 1572868
  332.8 16.2 %copy-start.4 = (bf16[1,1024,2048]{2,1,0:T(8,128)(2,1)S(1)}, bf16[1,1024,2048]{2,1,0:T(8,128)(2,1)}, u32[]{:S(2)}) copy-start(bf16[1,1024,2048]{2,1,0:T(8,128)(2,1)} %param.17) | copy-start | bytes 12582916
  357.6 8.0 %copy-start.3 = (f32[256,4]{0,1:T(4,128)S(1)}, f32[256,4]{0,1:T(4,128)}, u32[]{:S(2)}) copy-start(f32[256,4]{0,1:T(4,128)} %param.15) | copy-start | bytes 12292
  357.6 100.3 %all-to-all-start.2 = ((bf16[16,96,2048]{2,1,0:T(8,128)(2,1)}), bf16[16,96,2048]{2,1,0:T(8,128)(2,1)}, u32[]{:S(2)}, u32[]{:S(2)}) async-start(bf16[16,96,2048]{2,1,0:T(8,128)(2,1)} %convolution_convert_fusion), calls=%async_computation.2 | async-start | bytes 12582912 | tf_op jit(solution)/shard_map/all_to_all | solution.py:111
Sparse Core Ops, SparseCore 0:
  9.5 90.3 all-gather.3
  108.8 96.3 all-gather.5
